TPU v7x, 32 devices: a whole 2x2x4 slice. The times are simulated.
32 devices in a mesh: grp: 4 (over y, core), rep: 8 (over z, x).
Axes of the slice: x: 2, y: 2, z: 4, core: 2. Of those that a mesh axis runs over, the one named last changes fastest.
Arguments:
- tokens: bfloat16 [32, 1024, 768], P(('grp', 'rep')), may hold values from -6 to 6
- segment_ids: int32 [32, 1024], P(('grp', 'rep')), may hold values from 0 to 2, as said below
- cotangent: bfloat16 [32, 1024, 768], P(('grp', 'rep')), may hold values from -6 to 6
- in_proj_master: float32 [768, 3352], P('grp'), may hold values from -0.21875 to 0.21875
- out_proj_master: float32 [1536, 768], P('grp'), may hold values from -0.15625 to 0.15625
- in_proj_error: float32 [8, 768, 3352], P('rep', 'grp'), may hold values from -6 to 6
- out_proj_error: float32 [8, 1536, 768], P('rep', 'grp'), may hold values from -6 to 6
- in_proj_moment: float32 [768, 3352], P('grp'), may hold values from -6 to 6
- out_proj_moment: float32 [1536, 768], P('grp'), may hold values from -6 to 6
- in_proj_start: float32 [4, 3352, 8], P('grp'), may hold values from -6 to 6
- out_proj_start: float32 [4, 768, 8], P('grp'), may hold values from -6 to 6
- conv_master: float32 [5, 1792], replicated, may hold values from -3 to 3
- conv_moment: float32 [5, 1792], replicated, may hold values from -6 to 6
- head_master: float32 [3, 24], replicated, may hold values from -8 to 2, as said below
- head_moment: float32 [3, 24], replicated, may hold values from -6 to 6
- norm_gain: float32 [768], replicated, may hold values from 0.5 to 1.5
- norm_gain_moment: float32 [768], replicated, may hold values from -6 to 6
- gate_gain: float32 [1536], replicated, may hold values from 0.5 to 1.5
- gate_gain_moment: float32 [1536], replicated, may hold values from -6 to 6
Outputs:
- output: bfloat16 [32, 1024, 768], P(('grp', 'rep'))
- input_grad: float32 [32, 1024, 768], P(('grp', 'rep'))
- in_proj_grad: float32 [8, 768, 3352], P('rep', 'grp')
- out_proj_grad: float32 [8, 1536, 768], P('rep', 'grp')
- in_proj_left: float32 [768, 8], P('grp')
- out_proj_left: float32 [1536, 8], P('grp')
- in_proj_right: float32 [4, 3352, 8], P('grp')
- out_proj_right: float32 [4, 768, 8], P('grp')
- in_proj_error_new: float32 [8, 768, 3352], P('rep', 'grp')
- out_proj_error_new: float32 [8, 1536, 768], P('rep', 'grp')
- in_proj_moment_new: float32 [768, 3352], P('grp')
- out_proj_moment_new: float32 [1536, 768], P('grp')
- in_proj_master_new: float32 [768, 3352], P('grp')
- out_proj_master_new: float32 [1536, 768], P('grp')
- conv_grad: float32 [5, 1792], replicated
- conv_moment_new: float32 [5, 1792], replicated
- conv_master_new: float32 [5, 1792], replicated
- head_grad: float32 [3, 24], replicated
- head_moment_new: float32 [3, 24], replicated
- head_master_new: float32 [3, 24], replicated
- norm_gain_grad: float32 [768], replicated
- norm_gain_moment_new: float32 [768], replicated
- norm_gain_new: float32 [768], replicated
- gate_gain_grad: float32 [1536], replicated
- gate_gain_moment_new: float32 [1536], replicated
- gate_gain_new: float32 [1536], replicated
Inputs may be any that keep to these rules, and one draw needn't show every extreme that they name: `segment_ids`: within each sequence the ids never fall and all 3 ids occur; each document has 204 to 512 tokens and one has exactly 512. `head_master`: row 0 is the step bias, row 1 the log of the decay rate, row 2 the skip gain.
All inputs are finite; a program needn't handle non-finite values.
Results may differ from a plain program's by a relative error of at most 0.011.
Values may be sent and summed in bfloat16 or wider, within the bound.
No kernel may reach another device: no remote copies, remote signals or barrier semaphores. Data moves between devices by JAX's collectives and lax.ppermute only.
A program may use at most 256 MiB of HBM per device.

v0:
```python
import jax
import jax.numpy as jnp
from jax import lax
from jax.sharding import PartitionSpec as P

HEADS = 24
HEADDIM = 64
STATE = 128
CONV = 4
SPAN = 256
INNER = 1536
CONVDIM = 1792
EPS = 1e-05
GS_EPS = 1e-06
MOMENTUM = 0.9
RATE = 0.01
HIGH = lax.Precision.HIGHEST


def prenorm(inputs, gain):
    return inputs * lax.rsqrt(jnp.mean(inputs * inputs, axis=-1, keepdims=True) + EPS) * gain


def conv_part(projected, conv_params, head_params, segments):
    gate_in = projected[:, :INNER]
    conv_in = projected[:, INNER : INNER + CONVDIM]
    raw_steps = projected[:, INNER + CONVDIM :]
    summed = jnp.broadcast_to(conv_params[CONV], conv_in.shape)
    for offset in range(CONV):
        tap_row = conv_params[CONV - 1 - offset]
        if offset == 0:
            summed = summed + tap_row * conv_in
        else:
            shifted = jnp.pad(conv_in[:-offset], ((offset, 0), (0, 0)))
            earlier = jnp.pad(segments[:-offset], (offset, 0), constant_values=-1)
            same_doc = (earlier == segments).astype(jnp.float32)
            summed = summed + tap_row * shifted * same_doc[:, None]
    active = jax.nn.silu(summed)
    step_sizes = jax.nn.softplus(raw_steps + head_params[0])
    return (gate_in, active, step_sizes)


def span_step(carry, block):
    state, last_doc = carry
    values, sizes, decay_log, in_b, out_c, docs = block
    positions = docs.shape[0]
    heads_vals = values.reshape(positions, HEADS, HEADDIM)
    cumul = jnp.cumsum(decay_log, axis=1)
    places = jnp.arange(positions)
    allowed = (places[:, None] >= places[None, :]) & (docs[:, None] == docs[None, :])
    spread = cumul[:, :, None] - cumul[:, None, :]
    mask_three = allowed[None, :, :]
    decays = jnp.where(mask_three, jnp.exp(jnp.where(mask_three, spread, 0.0)), 0.0)
    inner_prod = jnp.dot(out_c, in_b.T, precision=HIGH)
    mixing = inner_prod[None, :, :] * decays * sizes[:, None, :]
    local_out = jnp.einsum("hij,jhp->ihp", mixing, heads_vals, precision=HIGH)
    alive = (docs == last_doc).astype(jnp.float32)
    carried = jnp.einsum("in,hpn->ihp", out_c, state, precision=HIGH)
    carried = carried * (jnp.exp(cumul).T * alive[:, None])[:, :, None]
    tail_weight = (
        jnp.exp(cumul[:, -1:] - cumul) * (docs == docs[-1]).astype(jnp.float32)[None, :] * sizes
    )
    keep_rate = jnp.exp(cumul[:, -1]) * (docs[-1] == last_doc).astype(jnp.float32)
    added = jnp.einsum("jhp,jn->hpn", tail_weight.T[:, :, None] * heads_vals, in_b, precision=HIGH)
    new_state = state * keep_rate[:, None, None] + added
    return ((new_state, docs[-1]), (local_out + carried).reshape(positions, INNER))


def spanned_scan(values, sizes, decay_log, in_b, out_c, segments):
    length = values.shape[0]
    blocks = length // SPAN
    pieces = (
        values.reshape(blocks, SPAN, INNER),
        jnp.swapaxes(sizes.reshape(blocks, SPAN, HEADS), 1, 2),
        jnp.swapaxes(decay_log.reshape(blocks, SPAN, HEADS), 1, 2),
        in_b.reshape(blocks, SPAN, STATE),
        out_c.reshape(blocks, SPAN, STATE),
        segments.reshape(blocks, SPAN),
    )
    start = (jnp.zeros((HEADS, HEADDIM, STATE), jnp.float32), jnp.array(-1, jnp.int32))
    ended, outputs = lax.scan(jax.checkpoint(span_step), start, pieces)
    return outputs.reshape(length, INNER)


def mixer_part(active, step_sizes, gate_in, head_params, gate_gain, segments):
    values = active[:, :INNER]
    in_b = active[:, INNER : INNER + STATE]
    out_c = active[:, INNER + STATE :]
    decay_log = -step_sizes * jnp.exp(head_params[1])
    scanned = spanned_scan(values, step_sizes, decay_log, in_b, out_c, segments)
    skip_row = jnp.repeat(head_params[2], HEADDIM)
    result = scanned + skip_row[None, :] * values
    gated = result * jax.nn.silu(gate_in)
    return gated * lax.rsqrt(jnp.mean(gated * gated, axis=-1, keepdims=True) + EPS) * gate_gain


def orthogonal(matrix):
    columns = []
    for index in range(matrix.shape[1]):
        vector = matrix[:, index]
        for done in columns:
            vector = vector - jnp.sum(done * vector) * done
        vector = vector * lax.rsqrt(jnp.sum(vector * vector) + GS_EPS)
        columns.append(vector)
    return jnp.stack(columns, axis=1)


def contract_rows(left_mat, right_mat, precision_kind):
    return lax.dot_general(
        left_mat,
        right_mat,
        (((0,), (0,)), ((), ())),
        precision=precision_kind,
        preferred_element_type=jnp.float32,
    )


def plain_update(grad_sum, moment, master, replicas):
    moment_new = MOMENTUM * moment + grad_sum / replicas
    return (moment_new, master - RATE * moment_new)


def on_device(
    tokens,
    segment_ids,
    cotangent,
    in_proj_master,
    out_proj_master,
    in_proj_error,
    out_proj_error,
    in_proj_moment,
    out_proj_moment,
    in_proj_start,
    out_proj_start,
    conv_master,
    conv_moment,
    head_master,
    head_moment,
    norm_gain,
    norm_gain_moment,
    gate_gain,
    gate_gain_moment,
):
    replicas = lax.axis_size("rep")
    w_in, w_out = (
        lax.all_gather(in_proj_master.astype(jnp.bfloat16), "grp", axis=0, tiled=True),
        lax.all_gather(out_proj_master.astype(jnp.bfloat16), "grp", axis=0, tiled=True),
    )
    seq_count, seq_len, width = tokens.shape
    row_count = seq_count * seq_len
    inputs = tokens.astype(jnp.float32)
    normed, norm_back = jax.vjp(prenorm, inputs, norm_gain)
    normed_low = normed.astype(jnp.bfloat16).reshape(row_count, width)
    projected = jnp.dot(normed_low, w_in, preferred_element_type=jnp.float32).reshape(
        seq_count, seq_len, -1
    )

    def first_part(proj_all, conv_params, head_params):
        return jax.vmap(conv_part, in_axes=(0, None, None, 0))(
            proj_all, conv_params, head_params, segment_ids
        )

    (gate_in, active, step_sizes), first_back = jax.vjp(
        first_part, projected, conv_master, head_master
    )
    active_low = lax.optimization_barrier(active.astype(jnp.bfloat16)).astype(jnp.float32)

    def second_part(active_all, sizes_all, gates_all, head_params, out_gain):
        return jax.vmap(mixer_part, in_axes=(0, 0, 0, None, None, 0))(
            active_all, sizes_all, gates_all, head_params, out_gain, segment_ids
        )

    mixed, second_back = jax.vjp(
        second_part, active_low, step_sizes, gate_in, head_master, gate_gain
    )
    mixed_low = mixed.astype(jnp.bfloat16).reshape(row_count, INNER)
    branch = jnp.dot(mixed_low, w_out, preferred_element_type=jnp.float32)
    output = (inputs + branch.reshape(tokens.shape)).astype(jnp.bfloat16)
    cot_rows = cotangent.reshape(row_count, width)
    d_mixed = lax.dot_general(
        cot_rows, w_out, (((1,), (1,)), ((), ())), preferred_element_type=jnp.float32
    )
    out_local = contract_rows(mixed_low, cot_rows, None)
    d_active, d_sizes, d_gates, d_heads_two, d_gate_gain = second_back(d_mixed.reshape(mixed.shape))
    d_projected, d_conv, d_heads_one = first_back((d_gates, d_active, d_sizes))
    d_proj_low = d_projected.astype(jnp.bfloat16).reshape(row_count, -1)
    in_local = contract_rows(normed_low, d_proj_low, None)
    d_normed = lax.dot_general(
        d_proj_low, w_in, (((1,), (1,)), ((), ())), preferred_element_type=jnp.float32
    )
    d_inputs, d_norm_gain = norm_back(d_normed.reshape(normed.shape))
    input_grad = cotangent.astype(jnp.float32) + d_inputs
    in_shard, out_shard = (
        lax.psum_scatter(in_local, "grp", scatter_dimension=0, tiled=True),
        lax.psum_scatter(out_local, "grp", scatter_dimension=0, tiled=True),
    )
    d_heads = d_heads_one + d_heads_two
    whole_in = in_shard + in_proj_error[0]
    whole_out = out_shard + out_proj_error[0]
    left_in = jnp.dot(whole_in, in_proj_start[0], precision=HIGH)
    left_out = jnp.dot(whole_out, out_proj_start[0], precision=HIGH)
    conv_grad, head_grad, norm_gain_grad, gate_gain_grad = lax.psum(
        (d_conv, d_heads, d_norm_gain, d_gate_gain), ("grp", "rep")
    )
    left_in, left_out = lax.psum((left_in, left_out), "rep")
    hat_in = orthogonal(left_in)
    hat_out = orthogonal(left_out)
    right_in = contract_rows(whole_in, hat_in, HIGH)
    right_out = contract_rows(whole_out, hat_out, HIGH)
    right_in, right_out = lax.psum((right_in, right_out), "rep")
    right_in = right_in / replicas
    right_out = right_out / replicas
    approx_in = jnp.dot(hat_in, right_in.T, precision=HIGH)
    approx_out = jnp.dot(hat_out, right_out.T, precision=HIGH)
    in_mom = MOMENTUM * in_proj_moment + approx_in
    out_mom = MOMENTUM * out_proj_moment + approx_out
    in_new = in_proj_master - RATE * in_mom
    out_new = out_proj_master - RATE * out_mom
    conv_mom, conv_new = plain_update(conv_grad, conv_moment, conv_master, replicas)
    head_mom, head_new = plain_update(head_grad, head_moment, head_master, replicas)
    gain_mom, gain_new = plain_update(norm_gain_grad, norm_gain_moment, norm_gain, replicas)
    gate_mom, gate_new = plain_update(gate_gain_grad, gate_gain_moment, gate_gain, replicas)
    return (
        output,
        input_grad,
        in_shard[None],
        out_shard[None],
        hat_in,
        hat_out,
        right_in[None],
        right_out[None],
        (whole_in - approx_in)[None],
        (whole_out - approx_out)[None],
        in_mom,
        out_mom,
        in_new,
        out_new,
        conv_grad,
        conv_mom,
        conv_new,
        head_grad,
        head_mom,
        head_new,
        norm_gain_grad,
        gain_mom,
        gain_new,
        gate_gain_grad,
        gate_mom,
        gate_new,
    )


def solution(mesh):
    return jax.shard_map(
        on_device,
        mesh=mesh,
        in_specs=(
            P(("grp", "rep"), None, None),
            P(("grp", "rep"), None),
            P(("grp", "rep"), None, None),
            P("grp", None),
            P("grp", None),
            P("rep", "grp", None),
            P("rep", "grp", None),
            P("grp", None),
            P("grp", None),
            P("grp", None, None),
            P("grp", None, None),
            P(),
            P(),
            P(),
            P(),
            P(),
            P(),
            P(),
            P(),
        ),
        out_specs=(
            P(("grp", "rep"), None, None),
            P(("grp", "rep"), None, None),
            P("rep", "grp", None),
            P("rep", "grp", None),
            P("grp", None),
            P("grp", None),
            P("grp", None, None),
            P("grp", None, None),
            P("rep", "grp", None),
            P("rep", "grp", None),
            P("grp", None),
            P("grp", None),
            P("grp", None),
            P("grp", None),
            P(),
            P(),
            P(),
            P(),
            P(),
            P(),
            P(),
            P(),
            P(),
            P(),
            P(),
            P(),
        ),
        check_vma=False,
    )
```

profile of v0, /device:TPU:0, one launch (start us, length us, event | category | flops | bytes accessed | tf_op | source)
XLA Modules:
  0.0 1407.3 jit_solution(13596165531728517373)
XLA Ops:
  14.2 39.9 %all-gather.3.cloned.1.call-done = bf16[768,3352]{1,0:T(8,128)(2,1)} async-done(((bf16[192,3352]{1,0:T(8,128)(2,1)}), bf16[768,3352]{1,0:T(8,128)(2,1)}) %all-gather.3.cloned.1.call-update) | async-done | bytes 5148688 | tf_op jit(solution)/shard_map/all_gather | solution.py:146
  75.4 15.0 %multiply_convert_fusion = (bf16[1,1024,1792]{1,2,0:T(8,128)(2,1)S(1)}, f32[1,1024,1792]{1,2,0:T(8,128)}) fusion(f32[1024]{0:T(1024)S(1)} %bitcast.693, f32[1,1021,1792]{1,2,0:T(8,128)} %slice.251, f32[1792]{0:T(1024)S(1)} %get-tuple-element.791, f32[1024]{0:T(1024)S(1)} %bitcast.691, f32[1,1022,1792]{1,2,0:T(8,128)} %slice.250, ...), kind=kLoop, calls=%fused_computation.159 | loop fusion | flops 29360128 | bytes 40375296 | tf_op jit(solution)/shard_map/convert_element_type | solution.py:166
  108.7 254.1 %while.46 = (s32[]{:T(128)}, f32[1,24,64,128]{3,2,1,0:T(8,128)S(1)}, s32[1]{0:T(128)}, f32[4,1,256,1536]{2,0,3,1:T(4,128)}, f32[4,1,24,64,128]{4,3,2,1,0:T(8,128...) while((s32[]{:T(128)}, ...), condition=%wide.region_4.5_spmd.clone, body=%wide.region_1.4_spmd.clone.sunk | while | flops 2527624192 | bytes 27957864 | solution.py:81
  137.4 34.2 %dynamic_update_slice.88 = f32[4,1,256,1536]{2,0,3,1:T(4,128)} dynamic-update-slice(f32[4,1,256,1536]{2,0,3,1:T(4,128)} %get-tuple-element.1300, f32[1,1,256,1536]{2,0,3,1:T(1,128)S(1)} %copy.412, s32[]{:T(128)S(6)} %copy.447, s32[]{:T(128)} %constant.161.clone.1..sunk, s32[]{:T(128)} %constant.161.clone.1..sunk, s32[]{:T(128)} %constant.161.clone.1..sunk) | dynamic-update-slice | bytes 3145732 | tf_op jit(solution)/shard_map/jvp(vmap())/while/body/jit(dynamic_update_index_in_dim)/dynamic_update_slice | solution.py:81
  200.9 34.2 %dynamic_update_slice.88 = f32[4,1,256,1536]{2,0,3,1:T(4,128)} dynamic-update-slice(f32[4,1,256,1536]{2,0,3,1:T(4,128)} %get-tuple-element.1300, f32[1,1,256,1536]{2,0,3,1:T(1,128)S(1)} %copy.412, s32[]{:T(128)S(6)} %copy.447, s32[]{:T(128)} %constant.161.clone.1..sunk, s32[]{:T(128)} %constant.161.clone.1..sunk, s32[]{:T(128)} %constant.161.clone.1..sunk) | dynamic-update-slice | bytes 3145732 | tf_op jit(solution)/shard_map/jvp(vmap())/while/body/jit(dynamic_update_index_in_dim)/dynamic_update_slice | solution.py:81
  264.5 34.2 %dynamic_update_slice.88 = f32[4,1,256,1536]{2,0,3,1:T(4,128)} dynamic-update-slice(f32[4,1,256,1536]{2,0,3,1:T(4,128)} %get-tuple-element.1300, f32[1,1,256,1536]{2,0,3,1:T(1,128)S(1)} %copy.412, s32[]{:T(128)S(6)} %copy.447, s32[]{:T(128)} %constant.161.clone.1..sunk, s32[]{:T(128)} %constant.161.clone.1..sunk, s32[]{:T(128)} %constant.161.clone.1..sunk) | dynamic-update-slice | bytes 3145732 | tf_op jit(solution)/shard_map/jvp(vmap())/while/body/jit(dynamic_update_index_in_dim)/dynamic_update_slice | solution.py:81
  328.0 34.2 %dynamic_update_slice.88 = f32[4,1,256,1536]{2,0,3,1:T(4,128)} dynamic-update-slice(f32[4,1,256,1536]{2,0,3,1:T(4,128)} %get-tuple-element.1300, f32[1,1,256,1536]{2,0,3,1:T(1,128)S(1)} %copy.412, s32[]{:T(128)S(6)} %copy.447, s32[]{:T(128)} %constant.161.clone.1..sunk, s32[]{:T(128)} %constant.161.clone.1..sunk, s32[]{:T(128)} %constant.161.clone.1..sunk) | dynamic-update-slice | bytes 3145732 | tf_op jit(solution)/shard_map/jvp(vmap())/while/body/jit(dynamic_update_index_in_dim)/dynamic_update_slice | solution.py:81
  368.7 8.7 transpose.175
  392.5 8.6 fusion.88
  401.2 19.5 %multiply_reduce_fusion.8 = (f32[1536]{0:T(1024)}, f32[1,1024,1536]{1,2,0:T(8,128)}, f32[1,1024,1536]{1,2,0:T(8,128)}) fusion(f32[1,1024,1792]{1,2,0:T(8,128)} %convert_element_type.87, f32[1,1024,3352]{1,2,0:T(8,128)} %copy-done.1, f32[1,1024,1536]{1,2,0:T(8,128)} %copy-done.7, f32[1024]{0:T(1024)S(1)} %multiply_multiply_fusion.1, f32[1024]{0:T(1024)S(1)} %fusion.124, ...), kind=kLoop, calls=%fused_computation.170 | loop fusion | flops 33028608 | bytes 44066816 | tf_op jit(solution)/shard_map/transpose(jvp(vmap()))/reduce_sum | solution.py:92
  435.3 512.2 %while.47 = (s32[]{:T(128)}, f32[1,24,64,128]{3,2,1,0:T(8,128)S(1)}, f32[4,1,256,1536]{2,0,3,1:T(4,128)}, f32[4,1,24,256]{2,3,1,0:T(8,128)}, f32[4,1,24,256]{3,0...) while((s32[]{:T(128)}, ...), condition=%wide.region_20.21_spmd.clone, body=%wide.region_7.20_spmd.clone.sunk | while | flops 5775293440 | bytes 58667620 | solution.py:81
  471.0 12.0 fusion.249
  529.3 34.1 %dynamic_update_slice.92 = f32[4,1,256,1536]{2,0,3,1:T(4,128)} dynamic-update-slice(f32[4,1,256,1536]{2,0,3,1:T(4,128)} %get-tuple-element.1349, f32[1,1,256,1536]{2,0,3,1:T(1,128)S(1)} %copy.427, s32[]{:T(128)S(6)} %sub.1200, s32[]{:T(128)} %constant.161.clone.1..sunk.1, s32[]{:T(128)} %constant.161.clone.1..sunk.1, s32[]{:T(128)} %constant.161.clone.1..sunk.1) | dynamic-update-slice | bytes 3145732 | tf_op jit(solution)/shard_map/transpose(jvp(vmap()))/while/body/jit(dynamic_update_index_in_dim)/dynamic_update_slice | solution.py:81
  598.9 12.0 fusion.249
  657.3 34.1 %dynamic_update_slice.92 = f32[4,1,256,1536]{2,0,3,1:T(4,128)} dynamic-update-slice(f32[4,1,256,1536]{2,0,3,1:T(4,128)} %get-tuple-element.1349, f32[1,1,256,1536]{2,0,3,1:T(1,128)S(1)} %copy.427, s32[]{:T(128)S(6)} %sub.1200, s32[]{:T(128)} %constant.161.clone.1..sunk.1, s32[]{:T(128)} %constant.161.clone.1..sunk.1, s32[]{:T(128)} %constant.161.clone.1..sunk.1) | dynamic-update-slice | bytes 3145732 | tf_op jit(solution)/shard_map/transpose(jvp(vmap()))/while/body/jit(dynamic_update_index_in_dim)/dynamic_update_slice | solution.py:81
  726.8 12.0 fusion.249
  785.2 34.1 %dynamic_update_slice.92 = f32[4,1,256,1536]{2,0,3,1:T(4,128)} dynamic-update-slice(f32[4,1,256,1536]{2,0,3,1:T(4,128)} %get-tuple-element.1349, f32[1,1,256,1536]{2,0,3,1:T(1,128)S(1)} %copy.427, s32[]{:T(128)S(6)} %sub.1200, s32[]{:T(128)} %constant.161.clone.1..sunk.1, s32[]{:T(128)} %constant.161.clone.1..sunk.1, s32[]{:T(128)} %constant.161.clone.1..sunk.1) | dynamic-update-slice | bytes 3145732 | tf_op jit(solution)/shard_map/transpose(jvp(vmap()))/while/body/jit(dynamic_update_index_in_dim)/dynamic_update_slice | solution.py:81
  854.7 12.0 fusion.249
  913.1 34.1 %dynamic_update_slice.92 = f32[4,1,256,1536]{2,0,3,1:T(4,128)} dynamic-update-slice(f32[4,1,256,1536]{2,0,3,1:T(4,128)} %get-tuple-element.1349, f32[1,1,256,1536]{2,0,3,1:T(1,128)S(1)} %copy.427, s32[]{:T(128)S(6)} %sub.1200, s32[]{:T(128)} %constant.161.clone.1..sunk.1, s32[]{:T(128)} %constant.161.clone.1..sunk.1, s32[]{:T(128)} %constant.161.clone.1..sunk.1) | dynamic-update-slice | bytes 3145732 | tf_op jit(solution)/shard_map/transpose(jvp(vmap()))/while/body/jit(dynamic_update_index_in_dim)/dynamic_update_slice | solution.py:81
  969.8 13.0 multiply_reduce_fusion.7
  982.8 11.9 multiply_reduce_fusion.6
  1005.2 8.4 slice_multiply_fusion.2
  1013.7 14.6 %multiply_reduce_fusion.4 = (f32[1792]{0:T(1024)S(1)}, f32[1792]{0:T(1024)S(1)}, f32[1,1024,1792]{1,2,0:T(8,128)}) fusion(f32[1,1024,1792]{1,2,0:T(8,128)S(1)} %bitcast.641, f32[1,1024,3352]{1,2,0:T(8,128)} %copy-done.1, f32[1792]{0:T(1024)S(1)} %copy-done.34, f32[1,1023,1792]{1,2,0:T(8,128)} %slice_multiply_fusion, ...), kind=kLoop, calls=%fused_computation.154 | loop fusion | flops 12841472 | bytes 44018688 | tf_op jit(solution)/shard_map/transpose(jvp(vmap()))/reduce_sum | solution.py:32
  1028.4 15.2 %fusion.107 = f32[768,3352]{1,0:T(8,128)} fusion(bf16[1,1024,768]{2,1,0:T(8,128)(2,1)S(1)} %copy-done.13, f32[768]{0:T(1024)S(1)} %copy-done.50, f32[1024]{0:T(1024)S(1)} %copy-done.52, f32[1,1024,1536]{1,2,0:T(8,128)} %get-tuple-element.1023, f32[1,1024,1792]{1,2,0:T(8,128)} %get-tuple-element.1024, f32[1,1024,24]{1,2,0:T(8,128)S(1)} %get-tuple-element.931), kind=kOutput, calls=%fused_computation.210 | convolution fusion | flops 5285683200 | bytes 25607168 | tf_op jit(solution)/shard_map/dot_general | solution.py:109
  1045.9 14.0 fusion.94
  1059.9 41.2 %all-reduce.25 = (f32[5,1792]{1,0:T(8,128)S(1)}, f32[3,24]{1,0:T(4,128)S(1)}, f32[768]{0:T(1024)S(1)}, f32[1536]{0:T(1024)S(1)}) all-reduce(f32[5,1792]{1,0:T(8,128)S(1)} %pad_add_fusion, f32[3,24]{1,0:T(4,128)} %add_add_fusion.2, f32[768]{0:T(1024)} %get-tuple-element.785, ...), channel_id=1, replica_groups=mesh['grp'=4,'rep'=8] {'grp','rep'}, use_global_device_ids=true, to_apply=%region_105.106 | all-reduce | flops 11336 | bytes 90688 | tf_op jit(solution)/shard_map/psum | solution.py:202
  1120.3 37.0 %psum.57 = f32[384,8]{0,1:T(8,128)S(1)} all-reduce(f32[384,8]{0,1:T(8,128)S(1)} %fusion.118), channel_id=1, replica_groups=mesh['grp'=4,'rep'=8] {'rep'}, use_global_device_ids=true, to_apply=%region_61.62 | all-reduce | flops 3072 | bytes 24576 | tf_op jit(solution)/shard_map/psum | solution.py:205
  1200.7 17.7 %subtract_multiply_fusion.2 = (f32[384,1]{0,1:T(1,128)S(1)}, f32[384,1]{0,1:T(1,128)S(1)}, f32[384,1]{0,1:T(1,128)S(1)}, f32[384,1]{0,1:T(1,128)S(1)}, f32[384,1...) fusion(f32[384,1]{0,1:T(1,128)S(1)} %get-tuple-element.1004, f32[384,8]{0,1:T(8,128)S(1)} %psum.57, ...), kind=kLoop, calls=%fused_computation.318 | loop fusion | flops 24192 | bytes 23180 | tf_op jit(solution)/shard_map/mul | solution.py:103
  1224.9 33.4 %all-reduce.26 = (f32[192,8]{0,1:T(8,128)S(1)}, f32[768,8]{0,1:T(8,128)S(1)}) all-reduce(f32[192,8]{0,1:T(8,128)S(1)} %fusion.110, f32[768,8]{0,1:T(8,128)S(1)} %fusion.128), channel_id=1, replica_groups=mesh['grp'=4,'rep'=8] {'rep'}, use_global_device_ids=true, to_apply=%region_24.25 | all-reduce | flops 7680 | bytes 61440 | tf_op jit(solution)/shard_map/psum | solution.py:205
  1300.2 17.6 %subtract_multiply_fusion.9 = (f32[192,1]{0,1:T(1,128)S(1)}, f32[192,1]{0,1:T(1,128)S(1)}, f32[192,1]{0,1:T(1,128)S(1)}, f32[192,1]{0,1:T(1,128)S(1)}, f32[192,1...) fusion(f32[192,1]{0,1:T(1,128)S(1)} %get-tuple-element.1033, f32[]{:T(128)S(6)} %rsqrt.79, ...), kind=kLoop, calls=%fused_computation.331 | loop fusion | flops 12096 | bytes 11660 | tf_op jit(solution)/shard_map/mul | solution.py:103
  1328.1 61.1 %all-reduce.29.cloned.1.call-done = f32[3352,8]{0,1:T(8,128)} async-done(((f32[3352,8]{0,1:T(8,128)}), f32[3352,8]{0,1:T(8,128)}) %all-reduce.29.cloned.1.call-update) | async-done | bytes 107280 | tf_op jit(solution)/shard_map/psum | solution.py:210
  1390.7 9.6 multiply_subtract_fusion
  (685 shorter events, 661.5 us)
Async XLA Ops:
  7.2 1213.6 %copy-start = (f32[1,3352,8]{1,2,0:T(8,128)S(1)}, f32[1,3352,8]{1,2,0:T(8,128)}, u32[]{:S(2)}) copy-start(f32[1,3352,8]{1,2,0:T(8,128)} %param.32) | copy-start | bytes 321796
  7.3 46.8 %copy-start.49 = (f32[768]{0:T(1024)S(1)}, f32[768]{0:T(1024)}, u32[]{:S(2)}) copy-start(f32[768]{0:T(1024)} %param.38) | copy-start | bytes 9220
  7.3 46.8 %all-gather.3.cloned.1.call-start = ((), (), s32[]{:S(2)}) async-start(), calls=%async_computation.2 | async-start | bytes 6635520 | tf_op jit(solution)/shard_map/all_gather | solution.py:146
  10.4 382.1 %all-gather.5.cloned.1.call-start = ((), (), s32[]{:S(2)}) async-start(), calls=%async_computation.3 | async-start | bytes 2949120 | tf_op jit(solution)/shard_map/all_gather | solution.py:147
  12.6 1104.8 %reduce-scatter.5.cloned.1.call-start = ((), (), s32[]{:S(2)}) async-start(), calls=%async_computation.5 | async-start | bytes 5898240 | tf_op jit(solution)/shard_map/reduce_scatter | solution.py:195
  12.8 81.5 %copy-start.58 = (f32[24]{0:T(128)}, f32[24]{0:T(128)S(1)}, u32[]{:S(2)}) copy-start(f32[24]{0:T(128)S(1)} %get-tuple-element.1044) | copy-start | bytes 292
  12.8 81.5 %copy-start.60 = (f32[24]{0:T(128)}, f32[24]{0:T(128)S(1)}, u32[]{:S(2)}) copy-start(f32[24]{0:T(128)S(1)} %get-tuple-element.1045) | copy-start | bytes 292
  13.7 48.7 %copy-start.51 = (f32[1024]{0:T(1024)}, f32[1024]{0:T(1024)S(1)}, u32[]{:S(2)}) copy-start(f32[1024]{0:T(1024)S(1)} %fusion.123) | copy-start | bytes 12292
  13.9 387.3 %copy-start.23 = (f32[1536]{0:T(1024)}, f32[1536]{0:T(1024)S(1)}, u32[]{:S(2)}) copy-start(f32[1536]{0:T(1024)S(1)} %mul.2216) | copy-start | bytes 18436
  14.0 61.4 %copy-start.27 = (f32[1792]{0:T(1024)}, f32[1792]{0:T(1024)S(1)}, u32[]{:S(2)}) copy-start(f32[1792]{0:T(1024)S(1)} %get-tuple-element.791) | copy-start | bytes 21508
  14.0 61.4 %copy-start.29 = (f32[1792]{0:T(1024)}, f32[1792]{0:T(1024)S(1)}, u32[]{:S(2)}) copy-start(f32[1792]{0:T(1024)S(1)} %get-tuple-element.789) | copy-start | bytes 21508
  14.0 61.4 %copy-start.31 = (f32[1792]{0:T(1024)}, f32[1792]{0:T(1024)S(1)}, u32[]{:S(2)}) copy-start(f32[1792]{0:T(1024)S(1)} %get-tuple-element.788) | copy-start | bytes 21508
  14.0 61.4 %copy-start.33 = (f32[1792]{0:T(1024)}, f32[1792]{0:T(1024)S(1)}, u32[]{:S(2)}) copy-start(f32[1792]{0:T(1024)S(1)} %get-tuple-element.790) | copy-start | bytes 21508
  14.1 61.2 %copy-start.37 = (f32[1,1024]{1,0:T(1,128)}, f32[1,1024]{1,0:T(1,128)S(1)}, u32[]{:S(2)}) copy-start(f32[1,1024]{1,0:T(1,128)S(1)} %get-tuple-element.1040) | copy-start | bytes 12292
  14.1 61.2 %copy-start.39 = (f32[1,1024]{1,0:T(1,128)}, f32[1,1024]{1,0:T(1,128)S(1)}, u32[]{:S(2)}) copy-start(f32[1,1024]{1,0:T(1,128)S(1)} %get-tuple-element.1041) | copy-start | bytes 12292
  14.2 61.2 %copy-start.43 = (f32[1,1024]{1,0:T(1,128)}, f32[1,1024]{1,0:T(1,128)S(1)}, u32[]{:S(2)}) copy-start(f32[1,1024]{1,0:T(1,128)S(1)} %get-tuple-element.1042) | copy-start | bytes 12292
  62.4 31.9 %copy-start.1 = (f32[1,1024,3352]{1,2,0:T(8,128)}, f32[1,1024,3352]{1,2,0:T(8,128)S(1)}, u32[]{:S(2)}) copy-start(f32[1,1024,3352]{1,2,0:T(8,128)S(1)} %convolution_bitcast_fusion.5) | copy-start | bytes 41189380
  401.1 819.6 %reduce-scatter.3.cloned.1.call-start = ((), (), s32[]{:S(2)}) async-start(), calls=%async_computation.4 | async-start | bytes 13271040 | tf_op jit(solution)/shard_map/reduce_scatter | solution.py:194
  438.6 18.3 %copy-start.3 = (f32[1,24,256]{1,2,0:T(8,128)}, f32[1,24,256]{1,2,0:T(8,128)S(1)}, u32[]{:S(2)}) copy-start(f32[1,24,256]{1,2,0:T(8,128)S(1)} %dynamic-slice_bitcast_fusion.11) | copy-start | bytes 73732 | tf_op jit(solution)/shard_map/transpose(jvp(vmap()))/while
  566.5 18.3 %copy-start.3 = (f32[1,24,256]{1,2,0:T(8,128)}, f32[1,24,256]{1,2,0:T(8,128)S(1)}, u32[]{:S(2)}) copy-start(f32[1,24,256]{1,2,0:T(8,128)S(1)} %dynamic-slice_bitcast_fusion.11) | copy-start | bytes 73732 | tf_op jit(solution)/shard_map/transpose(jvp(vmap()))/while
  822.4 18.3 %copy-start.3 = (f32[1,24,256]{1,2,0:T(8,128)}, f32[1,24,256]{1,2,0:T(8,128)S(1)}, u32[]{:S(2)}) copy-start(f32[1,24,256]{1,2,0:T(8,128)S(1)} %dynamic-slice_bitcast_fusion.11) | copy-start | bytes 73732 | tf_op jit(solution)/shard_map/transpose(jvp(vmap()))/while
  1043.6 345.6 %all-reduce.29.cloned.1.call-start = ((), (), s32[]{:S(2)}) async-start(), calls=%async_computation.6 | async-start | bytes 221184 | tf_op jit(solution)/shard_map/psum | solution.py:210
  1045.8 56.8 %copy-start.42 = (f32[1024]{0:T(1024)S(1)}, f32[1024]{0:T(1024)}, u32[]{:S(2)}) copy-start(f32[1024]{0:T(1024)} %copy-done.41) | copy-start | bytes 12292
  1045.8 58.8 %copy-start.46 = (f32[1536]{0:T(1024)S(1)}, f32[1536]{0:T(1024)}, u32[]{:S(2)}) copy-start(f32[1536]{0:T(1024)} %param.40) | copy-start | bytes 18436
  1045.8 58.8 %copy-start.55 = (f32[1536]{0:T(1024)S(1)}, f32[1536]{0:T(1024)}, u32[]{:S(2)}) copy-start(f32[1536]{0:T(1024)} %param.41) | copy-start | bytes 18436
  1045.9 59.4 %copy-start.22 = (f32[5,1792]{1,0:T(8,128)S(1)}, f32[5,1792]{1,0:T(8,128)}, u32[]{:S(2)}) copy-start(f32[5,1792]{1,0:T(8,128)} %param.34) | copy-start | bytes 107524
  1045.9 59.4 %copy-start.35 = (f32[5,1792]{1,0:T(8,128)S(1)}, f32[5,1792]{1,0:T(8,128)}, u32[]{:S(2)}) copy-start(f32[5,1792]{1,0:T(8,128)} %param.35) | copy-start | bytes 107524
  1045.9 60.0 %copy-start.15 = (bf16[1,1024,768]{2,1,0:T(8,128)(2,1)S(1)}, bf16[1,1024,768]{2,1,0:T(8,128)(2,1)}, u32[]{:S(2)}) copy-start(bf16[1,1024,768]{2,1,0:T(8,128)(2,1)} %param.25) | copy-start | bytes 4718596
  1059.9 50.5 %copy-start.54 = (f32[1024]{0:T(1024)S(1)}, f32[1024]{0:T(1024)}, u32[]{:S(2)}) copy-start(f32[1024]{0:T(1024)} %copy-done.53) | copy-start | bytes 12292
  1117.4 103.4 %copy-start.8 = (f32[1,192,3352]{2,1,0:T(8,128)S(1)}, f32[1,192,3352]{2,1,0:T(8,128)}, u32[]{:S(2)}) copy-start(f32[1,192,3352]{2,1,0:T(8,128)} %param.28) | copy-start | bytes 7723012
  1218.4 103.5 %copy-start.25 = (f32[384,8]{0,1:T(8,128)}, f32[384,8]{0,1:T(8,128)S(1)}, u32[]{:S(2)}) copy-start(f32[384,8]{0,1:T(8,128)S(1)} %stack.5) | copy-start | bytes 36868
  1317.8 72.9 %copy-start.26 = (f32[192,8]{0,1:T(8,128)}, f32[192,8]{0,1:T(8,128)S(1)}, u32[]{:S(2)}) copy-start(f32[192,8]{0,1:T(8,128)S(1)} %stack.4) | copy-start | bytes 18436
  (64 other events, 628.5 us)
Sparse Core Ops, SparseCore 0:
  10.5 43.4 all-gather.2
  56.2 24.0 all-gather.4
  401.3 47.9 reduce-scatter.4
  1043.7 85.9 reduce-scatter.2
  1322.0 67.0 all-reduce.28
where the time goes:
time: 1430 us; the launch traced here: 1410 us
  local copies, waits for them, and re-layouts  541 us (38%)
  other arithmetic  333 us (23%)
  matrix products  282 us (20%)
  blocking collectives  112 us (8%)
  waiting for transfers between devices  101 us (7%)
  between operations  25.8 us (2%)
    dynamic_update_slice x32, local copies, waits for them, and re-layouts, spanned_scan(): ended, outputs = lax.scan(jax.checkpoint(span_step), start, pieces)  352 us
    dot_general x12, matrix products, span_step(): local_out = jnp.einsum('hij,jhp->ihp', mixing, heads_vals, precision=HIGH)  107 us
    psum x2, blocking collectives, on_device(): left_in, left_out = lax.psum((left_in, left_out), 'rep')  70.4 us
    psum x1, waiting for transfers between devices, on_device(): right_in, right_out = lax.psum((right_in, right_out), 'rep')  61.1 us
    reduce_sum x20, other arithmetic, orthogonal(): vector = vector - jnp.sum(done * vector) * done  58.9 us
    psum x1, blocking collectives, on_device(): lax.psum((d_conv, d_heads, d_norm_gain, d_gate_gain), ('grp', 'rep'))  41.2 us
    all_gather x1, waiting for transfers between devices, on_device(): lax.all_gather(in_proj_master.astype(jnp.bfloat16), 'grp', axis=0, tiled=...  39.9 us
    dot_general x16, matrix products, span_step(): carried = jnp.einsum('in,hpn->ihp', out_c, state, precision=HIGH)  39.5 us
  transfers between devices with their start and end apart: 5, of which 2 were waited for; matrix products, arithmetic and copies ran while one was open for 76% of the time, Pallas kernels for 0%

commit v1 on v0

--- a/solution.py
+++ b/solution.py
@@ -15,6 +15,11 @@
 MOMENTUM = 0.9
 RATE = 0.01
 HIGH = lax.Precision.HIGHEST
+
+
+def swapped_in(value, axis, along):
+    sent = jnp.stack([value] * lax.axis_size(axis))
+    return jnp.concatenate(lax.all_to_all(sent, axis, 0, 0), axis=along)
 
 
 def prenorm(inputs, gain):
@@ -143,7 +148,7 @@
 ):
     replicas = lax.axis_size("rep")
     w_in, w_out = (
-        lax.all_gather(in_proj_master.astype(jnp.bfloat16), "grp", axis=0, tiled=True),
+        swapped_in(in_proj_master.astype(jnp.bfloat16), "grp", 0),
         lax.all_gather(out_proj_master.astype(jnp.bfloat16), "grp", axis=0, tiled=True),
     )
     seq_count, seq_len, width = tokens.shape

time: 1430 us -> 1470 us (1.028)
  waiting for transfers between devices: 101 us -> 131 us
    all_to_all x0 -> x1, waiting for transfers between devices: none -> 69.7 us  [swapped_in(): return jnp.concatenate(lax.all_to_all(sent, axis, 0, 0), axis=along)]
    all_gather x1 -> x0, waiting for transfers between devices: 39.9 us -> none  [on_device(): lax.all_gather(in_proj_master.astype(jnp.bfloat16), 'grp', axis=0, tiled=...]
    another operation x90 -> x91, local copies, waits for them, and re-layouts: 32.3 us -> 35 us
  transfers between devices with their start and end apart: 5 -> 5, of which waited for: 2 -> 2; matrix products, arithmetic and copies ran while one was open for 76% -> 74% of each run, Pallas kernels for 0% -> 0%
where the time goes in v1:
time: 1470 us; the launch traced here: 1440 us
  local copies, waits for them, and re-layouts  543 us (37%)
  other arithmetic  331 us (23%)
  matrix products  281 us (19%)
  waiting for transfers between devices  131 us (9%)
  blocking collectives  114 us (8%)
  between operations  25.8 us (2%)
    dynamic_update_slice x32, local copies, waits for them, and re-layouts, spanned_scan(): ended, outputs = lax.scan(jax.checkpoint(span_step), start, pieces)  352 us
    dot_general x12, matrix products, span_step(): local_out = jnp.einsum('hij,jhp->ihp', mixing, heads_vals, precision=HIGH)  107 us
    psum x2, blocking collectives, on_device(): left_in, left_out = lax.psum((left_in, left_out), 'rep')  70.4 us
    all_to_all x1, waiting for transfers between devices, swapped_in(): return jnp.concatenate(lax.all_to_all(sent, axis, 0, 0), axis=along)  69.7 us
    psum x1, waiting for transfers between devices, on_device(): right_in, right_out = lax.psum((right_in, right_out), 'rep')  61.1 us
    reduce_sum x20, other arithmetic, orthogonal(): vector = vector - jnp.sum(done * vector) * done  58.9 us
    psum x1, blocking collectives, on_device(): lax.psum((d_conv, d_heads, d_norm_gain, d_gate_gain), ('grp', 'rep'))  43.9 us
    dot_general x16, matrix products, span_step(): carried = jnp.einsum('in,hpn->ihp', out_c, state, precision=HIGH)  39.5 us
  transfers between devices with their start and end apart: 5, of which 2 were waited for; matrix products, arithmetic and copies ran while one was open for 74% of the time, Pallas kernels for 0%

profile of v1, /device:TPU:0, one launch (start us, length us, event | category | flops | bytes accessed | tf_op | source)
XLA Modules:
  0.0 1444.7 jit_solution(7421602638242624870)
XLA Ops:
  20.8 69.7 %all-to-all-done = bf16[4,192,3352]{2,1,0:T(8,128)(2,1)} async-done(((bf16[4,192,3352]{2,1,0:T(8,128)(2,1)}), bf16[4,192,3352]{2,1,0:T(8,128)(2,1)}, u32[]{:S(2)}, u32[]{:S(2)}) %all-to-all-start) | async-done | bytes 5148704 | tf_op jit(solution)/shard_map/all_to_all | solution.py:22
  111.9 15.0 %multiply_convert_fusion = (bf16[1,1024,1792]{1,2,0:T(8,128)(2,1)S(1)}, f32[1,1024,1792]{1,2,0:T(8,128)}) fusion(f32[1024]{0:T(1024)S(1)} %bitcast.694, f32[1,1021,1792]{1,2,0:T(8,128)} %slice.251, f32[1792]{0:T(1024)S(1)} %get-tuple-element.791, f32[1024]{0:T(1024)S(1)} %bitcast.692, f32[1,1022,1792]{1,2,0:T(8,128)} %slice.250, ...), kind=kLoop, calls=%fused_computation.159 | loop fusion | flops 29360128 | bytes 40375296 | tf_op jit(solution)/shard_map/convert_element_type | solution.py:171
  145.2 254.0 %while.46 = (s32[]{:T(128)}, f32[1,24,64,128]{3,2,1,0:T(8,128)S(1)}, s32[1]{0:T(128)}, f32[4,1,256,1536]{2,0,3,1:T(4,128)}, f32[4,1,24,64,128]{4,3,2,1,0:T(8,128...) while((s32[]{:T(128)}, ...), condition=%wide.region_4.5_spmd.clone, body=%wide.region_1.4_spmd.clone.sunk | while | flops 2527624192 | bytes 27957864 | solution.py:86
  173.9 34.1 %dynamic_update_slice.88 = f32[4,1,256,1536]{2,0,3,1:T(4,128)} dynamic-update-slice(f32[4,1,256,1536]{2,0,3,1:T(4,128)} %get-tuple-element.1300, f32[1,1,256,1536]{2,0,3,1:T(1,128)S(1)} %copy.412, s32[]{:T(128)S(6)} %copy.447, s32[]{:T(128)} %constant.161.clone.1..sunk, s32[]{:T(128)} %constant.161.clone.1..sunk, s32[]{:T(128)} %constant.161.clone.1..sunk) | dynamic-update-slice | bytes 3145732 | tf_op jit(solution)/shard_map/jvp(vmap())/while/body/jit(dynamic_update_index_in_dim)/dynamic_update_slice | solution.py:86
  237.4 34.1 %dynamic_update_slice.88 = f32[4,1,256,1536]{2,0,3,1:T(4,128)} dynamic-update-slice(f32[4,1,256,1536]{2,0,3,1:T(4,128)} %get-tuple-element.1300, f32[1,1,256,1536]{2,0,3,1:T(1,128)S(1)} %copy.412, s32[]{:T(128)S(6)} %copy.447, s32[]{:T(128)} %constant.161.clone.1..sunk, s32[]{:T(128)} %constant.161.clone.1..sunk, s32[]{:T(128)} %constant.161.clone.1..sunk) | dynamic-update-slice | bytes 3145732 | tf_op jit(solution)/shard_map/jvp(vmap())/while/body/jit(dynamic_update_index_in_dim)/dynamic_update_slice | solution.py:86
  300.9 34.1 %dynamic_update_slice.88 = f32[4,1,256,1536]{2,0,3,1:T(4,128)} dynamic-update-slice(f32[4,1,256,1536]{2,0,3,1:T(4,128)} %get-tuple-element.1300, f32[1,1,256,1536]{2,0,3,1:T(1,128)S(1)} %copy.412, s32[]{:T(128)S(6)} %copy.447, s32[]{:T(128)} %constant.161.clone.1..sunk, s32[]{:T(128)} %constant.161.clone.1..sunk, s32[]{:T(128)} %constant.161.clone.1..sunk) | dynamic-update-slice | bytes 3145732 | tf_op jit(solution)/shard_map/jvp(vmap())/while/body/jit(dynamic_update_index_in_dim)/dynamic_update_slice | solution.py:86
  364.5 34.1 %dynamic_update_slice.88 = f32[4,1,256,1536]{2,0,3,1:T(4,128)} dynamic-update-slice(f32[4,1,256,1536]{2,0,3,1:T(4,128)} %get-tuple-element.1300, f32[1,1,256,1536]{2,0,3,1:T(1,128)S(1)} %copy.412, s32[]{:T(128)S(6)} %copy.447, s32[]{:T(128)} %constant.161.clone.1..sunk, s32[]{:T(128)} %constant.161.clone.1..sunk, s32[]{:T(128)} %constant.161.clone.1..sunk) | dynamic-update-slice | bytes 3145732 | tf_op jit(solution)/shard_map/jvp(vmap())/while/body/jit(dynamic_update_index_in_dim)/dynamic_update_slice | solution.py:86
  405.1 8.7 transpose.175
  428.9 8.6 fusion.88
  437.6 18.9 %multiply_reduce_fusion.8 = (f32[1536]{0:T(1024)}, f32[1,1024,1536]{1,2,0:T(8,128)}, f32[1,1024,1536]{1,2,0:T(8,128)}) fusion(f32[1,1024,1792]{1,2,0:T(8,128)} %convert_element_type.87, f32[1,1024,3352]{1,2,0:T(8,128)} %copy-done.1, f32[1,1024,1536]{1,2,0:T(8,128)} %copy-done.7, f32[1024]{0:T(1024)S(1)} %multiply_multiply_fusion.1, f32[1024]{0:T(1024)S(1)} %fusion.124, ...), kind=kLoop, calls=%fused_computation.170 | loop fusion | flops 33028608 | bytes 44066816 | tf_op jit(solution)/shard_map/transpose(jvp(vmap()))/reduce_sum | solution.py:97
  471.0 512.2 %while.47 = (s32[]{:T(128)}, f32[1,24,64,128]{3,2,1,0:T(8,128)S(1)}, f32[4,1,256,1536]{2,0,3,1:T(4,128)}, f32[4,1,24,256]{2,3,1,0:T(8,128)}, f32[4,1,24,256]{3,0...) while((s32[]{:T(128)}, ...), condition=%wide.region_20.21_spmd.clone, body=%wide.region_7.20_spmd.clone.sunk | while | flops 5775293440 | bytes 58667620 | solution.py:86
  506.7 12.0 fusion.249
  565.0 34.1 %dynamic_update_slice.92 = f32[4,1,256,1536]{2,0,3,1:T(4,128)} dynamic-update-slice(f32[4,1,256,1536]{2,0,3,1:T(4,128)} %get-tuple-element.1349, f32[1,1,256,1536]{2,0,3,1:T(1,128)S(1)} %copy.427, s32[]{:T(128)S(6)} %sub.1200, s32[]{:T(128)} %constant.161.clone.1..sunk.1, s32[]{:T(128)} %constant.161.clone.1..sunk.1, s32[]{:T(128)} %constant.161.clone.1..sunk.1) | dynamic-update-slice | bytes 3145732 | tf_op jit(solution)/shard_map/transpose(jvp(vmap()))/while/body/jit(dynamic_update_index_in_dim)/dynamic_update_slice | solution.py:86
  634.6 12.0 fusion.249
  693.0 34.1 %dynamic_update_slice.92 = f32[4,1,256,1536]{2,0,3,1:T(4,128)} dynamic-update-slice(f32[4,1,256,1536]{2,0,3,1:T(4,128)} %get-tuple-element.1349, f32[1,1,256,1536]{2,0,3,1:T(1,128)S(1)} %copy.427, s32[]{:T(128)S(6)} %sub.1200, s32[]{:T(128)} %constant.161.clone.1..sunk.1, s32[]{:T(128)} %constant.161.clone.1..sunk.1, s32[]{:T(128)} %constant.161.clone.1..sunk.1) | dynamic-update-slice | bytes 3145732 | tf_op jit(solution)/shard_map/transpose(jvp(vmap()))/while/body/jit(dynamic_update_index_in_dim)/dynamic_update_slice | solution.py:86
  762.5 12.0 fusion.249
  820.9 34.1 %dynamic_update_slice.92 = f32[4,1,256,1536]{2,0,3,1:T(4,128)} dynamic-update-slice(f32[4,1,256,1536]{2,0,3,1:T(4,128)} %get-tuple-element.1349, f32[1,1,256,1536]{2,0,3,1:T(1,128)S(1)} %copy.427, s32[]{:T(128)S(6)} %sub.1200, s32[]{:T(128)} %constant.161.clone.1..sunk.1, s32[]{:T(128)} %constant.161.clone.1..sunk.1, s32[]{:T(128)} %constant.161.clone.1..sunk.1) | dynamic-update-slice | bytes 3145732 | tf_op jit(solution)/shard_map/transpose(jvp(vmap()))/while/body/jit(dynamic_update_index_in_dim)/dynamic_update_slice | solution.py:86
  890.4 12.0 fusion.249
  948.8 34.1 %dynamic_update_slice.92 = f32[4,1,256,1536]{2,0,3,1:T(4,128)} dynamic-update-slice(f32[4,1,256,1536]{2,0,3,1:T(4,128)} %get-tuple-element.1349, f32[1,1,256,1536]{2,0,3,1:T(1,128)S(1)} %copy.427, s32[]{:T(128)S(6)} %sub.1200, s32[]{:T(128)} %constant.161.clone.1..sunk.1, s32[]{:T(128)} %constant.161.clone.1..sunk.1, s32[]{:T(128)} %constant.161.clone.1..sunk.1) | dynamic-update-slice | bytes 3145732 | tf_op jit(solution)/shard_map/transpose(jvp(vmap()))/while/body/jit(dynamic_update_index_in_dim)/dynamic_update_slice | solution.py:86
  1005.5 13.0 multiply_reduce_fusion.7
  1018.5 11.9 multiply_reduce_fusion.6
  1040.9 8.4 slice_multiply_fusion.2
  1049.4 14.6 %multiply_reduce_fusion.4 = (f32[1792]{0:T(1024)S(1)}, f32[1792]{0:T(1024)S(1)}, f32[1,1024,1792]{1,2,0:T(8,128)}) fusion(f32[1,1024,1792]{1,2,0:T(8,128)S(1)} %bitcast.642, f32[1,1024,3352]{1,2,0:T(8,128)} %copy-done.1, f32[1792]{0:T(1024)S(1)} %copy-done.34, f32[1,1023,1792]{1,2,0:T(8,128)} %slice_multiply_fusion, ...), kind=kLoop, calls=%fused_computation.154 | loop fusion | flops 12841472 | bytes 44018688 | tf_op jit(solution)/shard_map/transpose(jvp(vmap()))/reduce_sum | solution.py:37
  1064.1 15.2 %fusion.107 = f32[768,3352]{1,0:T(8,128)} fusion(bf16[1,1024,768]{2,1,0:T(8,128)(2,1)S(1)} %copy-done.13, f32[768]{0:T(1024)S(1)} %copy-done.50, f32[1024]{0:T(1024)S(1)} %copy-done.52, f32[1,1024,1536]{1,2,0:T(8,128)} %get-tuple-element.1023, f32[1,1024,1792]{1,2,0:T(8,128)} %get-tuple-element.1024, f32[1,1024,24]{1,2,0:T(8,128)S(1)} %get-tuple-element.931), kind=kOutput, calls=%fused_computation.210 | convolution fusion | flops 5285683200 | bytes 25607168 | tf_op jit(solution)/shard_map/dot_general | solution.py:114
  1081.6 13.0 fusion.94
  1094.6 43.9 %all-reduce.25 = (f32[5,1792]{1,0:T(8,128)S(1)}, f32[3,24]{1,0:T(4,128)S(1)}, f32[768]{0:T(1024)S(1)}, f32[1536]{0:T(1024)S(1)}) all-reduce(f32[5,1792]{1,0:T(8,128)S(1)} %pad_add_fusion, f32[3,24]{1,0:T(4,128)} %add_add_fusion.2, f32[768]{0:T(1024)} %get-tuple-element.785, ...), channel_id=1, replica_groups=mesh['grp'=4,'rep'=8] {'grp','rep'}, use_global_device_ids=true, to_apply=%region_105.106 | all-reduce | flops 11336 | bytes 90688 | tf_op jit(solution)/shard_map/psum | solution.py:207
  1157.7 37.0 %psum.57 = f32[384,8]{0,1:T(8,128)S(1)} all-reduce(f32[384,8]{0,1:T(8,128)S(1)} %fusion.118), channel_id=1, replica_groups=mesh['grp'=4,'rep'=8] {'rep'}, use_global_device_ids=true, to_apply=%region_61.62 | all-reduce | flops 3072 | bytes 24576 | tf_op jit(solution)/shard_map/psum | solution.py:210
  1238.0 17.7 %subtract_multiply_fusion.2 = (f32[384,1]{0,1:T(1,128)S(1)}, f32[384,1]{0,1:T(1,128)S(1)}, f32[384,1]{0,1:T(1,128)S(1)}, f32[384,1]{0,1:T(1,128)S(1)}, f32[384,1...) fusion(f32[384,1]{0,1:T(1,128)S(1)} %get-tuple-element.1004, f32[384,8]{0,1:T(8,128)S(1)} %psum.57, ...), kind=kLoop, calls=%fused_computation.318 | loop fusion | flops 24192 | bytes 23180 | tf_op jit(solution)/shard_map/mul | solution.py:108
  1262.3 33.4 %all-reduce.26 = (f32[192,8]{0,1:T(8,128)S(1)}, f32[768,8]{0,1:T(8,128)S(1)}) all-reduce(f32[192,8]{0,1:T(8,128)S(1)} %fusion.110, f32[768,8]{0,1:T(8,128)S(1)} %fusion.128), channel_id=1, replica_groups=mesh['grp'=4,'rep'=8] {'rep'}, use_global_device_ids=true, to_apply=%region_24.25 | all-reduce | flops 7680 | bytes 61440 | tf_op jit(solution)/shard_map/psum | solution.py:210
  1337.6 17.6 %subtract_multiply_fusion.9 = (f32[192,1]{0,1:T(1,128)S(1)}, f32[192,1]{0,1:T(1,128)S(1)}, f32[192,1]{0,1:T(1,128)S(1)}, f32[192,1]{0,1:T(1,128)S(1)}, f32[192,1...) fusion(f32[192,1]{0,1:T(1,128)S(1)} %get-tuple-element.1033, f32[]{:T(128)S(6)} %rsqrt.79, ...), kind=kLoop, calls=%fused_computation.331 | loop fusion | flops 12096 | bytes 11660 | tf_op jit(solution)/shard_map/mul | solution.py:108
  1365.5 61.1 %all-reduce.29.cloned.1.call-done = f32[3352,8]{0,1:T(8,128)} async-done(((f32[3352,8]{0,1:T(8,128)}), f32[3352,8]{0,1:T(8,128)}) %all-reduce.29.cloned.1.call-update) | async-done | bytes 107280 | tf_op jit(solution)/shard_map/psum | solution.py:215
  1428.1 9.6 multiply_subtract_fusion
  (685 shorter events, 668.1 us)
Async XLA Ops:
  7.2 1251.0 %copy-start = (f32[1,3352,8]{1,2,0:T(8,128)S(1)}, f32[1,3352,8]{1,2,0:T(8,128)}, u32[]{:S(2)}) copy-start(f32[1,3352,8]{1,2,0:T(8,128)} %param.32) | copy-start | bytes 321796
  11.8 78.7 %copy-start.49 = (f32[768]{0:T(1024)S(1)}, f32[768]{0:T(1024)}, u32[]{:S(2)}) copy-start(f32[768]{0:T(1024)} %param.38) | copy-start | bytes 9220
  11.8 78.7 %all-to-all-start = ((bf16[4,192,3352]{2,1,0:T(8,128)(2,1)}), bf16[4,192,3352]{2,1,0:T(8,128)(2,1)}, u32[]{:S(2)}, u32[]{:S(2)}) async-start(bf16[4,192,3352]{2,1,0:T(8,128)(2,1)} %stack.6), calls=%async_computation | async-start | bytes 10616832 | tf_op jit(solution)/shard_map/all_to_all | solution.py:22
  17.1 411.9 %all-gather.2.cloned.1.call-start = ((), (), s32[]{:S(2)}) async-start(), calls=%async_computation.3 | async-start | bytes 2949120 | tf_op jit(solution)/shard_map/all_gather | solution.py:152
  19.3 1135.5 %reduce-scatter.5.cloned.1.call-start = ((), (), s32[]{:S(2)}) async-start(), calls=%async_computation.5 | async-start | bytes 5898240 | tf_op jit(solution)/shard_map/reduce_scatter | solution.py:200
  19.4 111.4 %copy-start.58 = (f32[24]{0:T(128)}, f32[24]{0:T(128)S(1)}, u32[]{:S(2)}) copy-start(f32[24]{0:T(128)S(1)} %get-tuple-element.1044) | copy-start | bytes 292
  19.4 111.4 %copy-start.60 = (f32[24]{0:T(128)}, f32[24]{0:T(128)S(1)}, u32[]{:S(2)}) copy-start(f32[24]{0:T(128)S(1)} %get-tuple-element.1045) | copy-start | bytes 292
  19.6 418.0 %copy-start.23 = (f32[1536]{0:T(1024)}, f32[1536]{0:T(1024)S(1)}, u32[]{:S(2)}) copy-start(f32[1536]{0:T(1024)S(1)} %mul.2216) | copy-start | bytes 18436
  19.7 92.2 %copy-start.27 = (f32[1792]{0:T(1024)}, f32[1792]{0:T(1024)S(1)}, u32[]{:S(2)}) copy-start(f32[1792]{0:T(1024)S(1)} %get-tuple-element.791) | copy-start | bytes 21508
  19.7 92.2 %copy-start.29 = (f32[1792]{0:T(1024)}, f32[1792]{0:T(1024)S(1)}, u32[]{:S(2)}) copy-start(f32[1792]{0:T(1024)S(1)} %get-tuple-element.789) | copy-start | bytes 21508
  19.7 92.2 %copy-start.31 = (f32[1792]{0:T(1024)}, f32[1792]{0:T(1024)S(1)}, u32[]{:S(2)}) copy-start(f32[1792]{0:T(1024)S(1)} %get-tuple-element.788) | copy-start | bytes 21508
  19.7 92.2 %copy-start.33 = (f32[1792]{0:T(1024)}, f32[1792]{0:T(1024)S(1)}, u32[]{:S(2)}) copy-start(f32[1792]{0:T(1024)S(1)} %get-tuple-element.790) | copy-start | bytes 21508
  20.1 78.7 %copy-start.51 = (f32[1024]{0:T(1024)}, f32[1024]{0:T(1024)S(1)}, u32[]{:S(2)}) copy-start(f32[1024]{0:T(1024)S(1)} %fusion.123) | copy-start | bytes 12292
  20.8 91.1 %copy-start.37 = (f32[1,1024]{1,0:T(1,128)}, f32[1,1024]{1,0:T(1,128)S(1)}, u32[]{:S(2)}) copy-start(f32[1,1024]{1,0:T(1,128)S(1)} %get-tuple-element.1040) | copy-start | bytes 12292
  20.8 91.1 %copy-start.39 = (f32[1,1024]{1,0:T(1,128)}, f32[1,1024]{1,0:T(1,128)S(1)}, u32[]{:S(2)}) copy-start(f32[1,1024]{1,0:T(1,128)S(1)} %get-tuple-element.1041) | copy-start | bytes 12292
  20.8 91.1 %copy-start.43 = (f32[1,1024]{1,0:T(1,128)}, f32[1,1024]{1,0:T(1,128)S(1)}, u32[]{:S(2)}) copy-start(f32[1,1024]{1,0:T(1,128)S(1)} %get-tuple-element.1042) | copy-start | bytes 12292
  98.9 31.9 %copy-start.1 = (f32[1,1024,3352]{1,2,0:T(8,128)}, f32[1,1024,3352]{1,2,0:T(8,128)S(1)}, u32[]{:S(2)}) copy-start(f32[1,1024,3352]{1,2,0:T(8,128)S(1)} %convolution_bitcast_fusion.5) | copy-start | bytes 41189380
  437.5 820.6 %reduce-scatter.3.cloned.1.call-start = ((), (), s32[]{:S(2)}) async-start(), calls=%async_computation.4 | async-start | bytes 13271040 | tf_op jit(solution)/shard_map/reduce_scatter | solution.py:199
  474.3 18.3 %copy-start.3 = (f32[1,24,256]{1,2,0:T(8,128)}, f32[1,24,256]{1,2,0:T(8,128)S(1)}, u32[]{:S(2)}) copy-start(f32[1,24,256]{1,2,0:T(8,128)S(1)} %dynamic-slice_bitcast_fusion.11) | copy-start | bytes 73732 | tf_op jit(solution)/shard_map/transpose(jvp(vmap()))/while
  602.2 18.3 %copy-start.3 = (f32[1,24,256]{1,2,0:T(8,128)}, f32[1,24,256]{1,2,0:T(8,128)S(1)}, u32[]{:S(2)}) copy-start(f32[1,24,256]{1,2,0:T(8,128)S(1)} %dynamic-slice_bitcast_fusion.11) | copy-start | bytes 73732 | tf_op jit(solution)/shard_map/transpose(jvp(vmap()))/while
  858.1 18.3 %copy-start.3 = (f32[1,24,256]{1,2,0:T(8,128)}, f32[1,24,256]{1,2,0:T(8,128)S(1)}, u32[]{:S(2)}) copy-start(f32[1,24,256]{1,2,0:T(8,128)S(1)} %dynamic-slice_bitcast_fusion.11) | copy-start | bytes 73732 | tf_op jit(solution)/shard_map/transpose(jvp(vmap()))/while
  1079.3 347.2 %all-reduce.29.cloned.1.call-start = ((), (), s32[]{:S(2)}) async-start(), calls=%async_computation.6 | async-start | bytes 221184 | tf_op jit(solution)/shard_map/psum | solution.py:215
  1081.5 58.5 %copy-start.42 = (f32[1024]{0:T(1024)S(1)}, f32[1024]{0:T(1024)}, u32[]{:S(2)}) copy-start(f32[1024]{0:T(1024)} %copy-done.41) | copy-start | bytes 12292
  1081.5 60.5 %copy-start.46 = (f32[1536]{0:T(1024)S(1)}, f32[1536]{0:T(1024)}, u32[]{:S(2)}) copy-start(f32[1536]{0:T(1024)} %param.40) | copy-start | bytes 18436
  1081.5 60.5 %copy-start.55 = (f32[1536]{0:T(1024)S(1)}, f32[1536]{0:T(1024)}, u32[]{:S(2)}) copy-start(f32[1536]{0:T(1024)} %param.41) | copy-start | bytes 18436
  1081.6 61.1 %copy-start.22 = (f32[5,1792]{1,0:T(8,128)S(1)}, f32[5,1792]{1,0:T(8,128)}, u32[]{:S(2)}) copy-start(f32[5,1792]{1,0:T(8,128)} %param.34) | copy-start | bytes 107524
  1081.6 61.1 %copy-start.35 = (f32[5,1792]{1,0:T(8,128)S(1)}, f32[5,1792]{1,0:T(8,128)}, u32[]{:S(2)}) copy-start(f32[5,1792]{1,0:T(8,128)} %param.35) | copy-start | bytes 107524
  1081.6 61.7 %copy-start.15 = (bf16[1,1024,768]{2,1,0:T(8,128)(2,1)S(1)}, bf16[1,1024,768]{2,1,0:T(8,128)(2,1)}, u32[]{:S(2)}) copy-start(bf16[1,1024,768]{2,1,0:T(8,128)(2,1)} %param.25) | copy-start | bytes 4718596
  1094.6 53.2 %copy-start.54 = (f32[1024]{0:T(1024)S(1)}, f32[1024]{0:T(1024)}, u32[]{:S(2)}) copy-start(f32[1024]{0:T(1024)} %copy-done.53) | copy-start | bytes 12292
  1154.8 103.4 %copy-start.8 = (f32[1,192,3352]{2,1,0:T(8,128)S(1)}, f32[1,192,3352]{2,1,0:T(8,128)}, u32[]{:S(2)}) copy-start(f32[1,192,3352]{2,1,0:T(8,128)} %param.28) | copy-start | bytes 7723012
  1255.8 103.5 %copy-start.25 = (f32[384,8]{0,1:T(8,128)}, f32[384,8]{0,1:T(8,128)S(1)}, u32[]{:S(2)}) copy-start(f32[384,8]{0,1:T(8,128)S(1)} %stack.8) | copy-start | bytes 36868
  1355.2 72.9 %copy-start.26 = (f32[192,8]{0,1:T(8,128)}, f32[192,8]{0,1:T(8,128)S(1)}, u32[]{:S(2)}) copy-start(f32[192,8]{0,1:T(8,128)S(1)} %stack.7) | copy-start | bytes 18436
  (64 other events, 635.9 us)
Sparse Core Ops, SparseCore 0:
  20.0 39.9 all-gather.1
  437.7 49.0 reduce-scatter.4
  1079.4 87.7 reduce-scatter.2
  1359.4 67.0 all-reduce.28
